TPU v7x, 32 devices: a whole 2x2x4 slice. The times are simulated.
32 devices in a mesh: row: 8 (over z, x), col: 4 (over y, core).
Axes of the slice: x: 2, y: 2, z: 4, core: 2. Of those that a mesh axis runs over, the one named last changes fastest.
Arguments:
- layer_input: bfloat16 [16384, 960], P(('row', 'col')), may hold values from -6 to 6
- norm1_gain: float32 [960], replicated, may hold values from 0.5 to 1.5
- w_qkv: bfloat16 [960, 1600], P('row', 'col'), may hold values from -0.1875 to 0.1875
- w_out: bfloat16 [960, 960], P('row', 'col'), may hold values from -1.5 to 1.5
- norm2_gain: float32 [960], replicated, may hold values from 0.5 to 1.5
- w_gate: bfloat16 [960, 2560], P('row', 'col'), may hold values from -0.1875 to 0.1875
- w_up: bfloat16 [960, 2560], P('row', 'col'), may hold values from -0.1875 to 0.1875
- w_down: bfloat16 [960, 2560], P('row', 'col'), may hold values from -0.15625 to 0.15625
- out_cotangent: bfloat16 [16384, 960], P(('row', 'col')), may hold values from -6 to 6
- seq_lengths: int32 [8, 3], P('row'), may hold values from 1 to 1024, 2048 in all within a row
- position_ids: int32 [16384], P(('row', 'col')), may hold values from 0 to 4094, as said below
- deal_rows: int32 [32, 8], P(('row', 'col')), may hold values from 0 to 7, each once within a row
Outputs:
- layer_output: bfloat16 [16384, 960], P(('row', 'col'))
- grad_input: bfloat16 [16384, 960], P(('row', 'col'))
- grad_norm1: float32 [960], replicated
- grad_qkv: float32 [960, 1600], P('row', 'col')
- grad_out: float32 [960, 960], P('row', 'col')
- grad_norm2: float32 [960], replicated
- grad_gate: float32 [960, 2560], P('row', 'col')
- grad_up: float32 [960, 2560], P('row', 'col')
- grad_down: float32 [960, 2560], P('row', 'col')
Inputs may be any that keep to these rules, and one draw needn't show every extreme that they name: Each row of seq_lengths gives the lengths of the 3 sequences packed in order into one row group of 2048 dealt rows; each row sums to 2048, and its largest entry is exactly 1024. `position_ids`: within each aligned group of 2048 dealt rows the ids start at 0 and rise by 1 or 2 from one row to the next; in some group they rise by 2 at every row. `deal_rows`: each row is a permutation of the 8 row groups.
All inputs are finite; a program needn't handle non-finite values.
Results may differ from a plain program's by a relative error of at most 0.015.
Values may be sent and summed in bfloat16 or wider, within the bound.
A program may use at most 128 MiB of HBM per device.

v0:
```python
import math
import jax
import jax.numpy as jnp
from jax import lax
from jax.sharding import PartitionSpec as P

QUERY_HEADS = 15
KEY_VALUE_HEADS = 5
HEAD_DIMENSION = 64
QUERY_FEATURES = 960
KEY_FEATURES = 320
EPS = 1e-05
NEG_FILL = -1e30
THETA = 10000.0


def matmul(left_mat, right_mat):
    return jnp.dot(left_mat, right_mat, preferred_element_type=jnp.float32)


def matmul_nt(left_mat, right_mat):
    return lax.dot_general(
        left_mat, right_mat, (((1,), (1,)), ((), ())), preferred_element_type=jnp.float32
    )


def matmul_tn(left_mat, right_mat):
    return lax.dot_general(
        left_mat, right_mat, (((0,), (0,)), ((), ())), preferred_element_type=jnp.float32
    )


def rms_scale(values):
    return lax.rsqrt(jnp.mean(values * values, axis=1, keepdims=True) + EPS)


def rope_tables(position, head_size):
    half_size = head_size // 2
    inverse = jnp.exp(
        jnp.arange(half_size, dtype=jnp.float32) * (-2.0 * math.log(THETA) / head_size)
    )
    angles = position.astype(jnp.float32)[:, None] * inverse[None, :]
    return (jnp.cos(angles), jnp.sin(angles))


def apply_rotation(values, cosine_table, sine_table, head_count):
    pieces = values.reshape(values.shape[0], head_count, -1)
    half_size = pieces.shape[2] // 2
    first_half = pieces[:, :, :half_size]
    second_half = pieces[:, :, half_size:]
    cos_wide = cosine_table[:, None, :]
    sin_wide = sine_table[:, None, :]
    turned = jnp.concatenate(
        [
            first_half * cos_wide - second_half * sin_wide,
            second_half * cos_wide + first_half * sin_wide,
        ],
        axis=2,
    )
    return turned.reshape(values.shape)


def reverse_rotation(values, cosine_table, sine_table, head_count):
    pieces = values.reshape(values.shape[0], head_count, -1)
    half_size = pieces.shape[2] // 2
    first_half = pieces[:, :, :half_size]
    second_half = pieces[:, :, half_size:]
    cos_wide = cosine_table[:, None, :]
    sin_wide = sine_table[:, None, :]
    turned = jnp.concatenate(
        [
            first_half * cos_wide + second_half * sin_wide,
            second_half * cos_wide - first_half * sin_wide,
        ],
        axis=2,
    )
    return turned.reshape(values.shape)


def gather_rows(values):
    return lax.all_gather(values, "col", axis=0, tiled=True)


def regroup_tokens(values):
    return lax.all_to_all(values, "col", split_axis=0, concat_axis=1, tiled=True)


def regroup_columns(values):
    return lax.all_to_all(values, "col", split_axis=1, concat_axis=0, tiled=True)


def spread_sum(products, own_rows):
    result = jnp.zeros((lax.axis_size("col") * own_rows, products[0][1].shape[0]), jnp.float32)
    for left_mat, right_mat in products:
        result = result + matmul_nt(left_mat, right_mat)
    return lax.psum_scatter(result, "col", scatter_dimension=0, tiled=True)


def attend(query_heads, heads_of_key, heads_of_value, allowed, factor):
    heads_per_group = query_heads.shape[0] // heads_of_key.shape[0]

    def one_head(unused, element):
        query_rows, head_index = element
        key_rows = lax.dynamic_index_in_dim(
            heads_of_key, head_index // heads_per_group, 0, keepdims=False
        )
        value_rows = lax.dynamic_index_in_dim(
            heads_of_value, head_index // heads_per_group, 0, keepdims=False
        )
        scores = jnp.where(allowed, matmul_nt(query_rows, key_rows) * factor, NEG_FILL)
        row_max = jnp.max(scores, axis=1, keepdims=True)
        weights = jnp.exp(scores - row_max)
        row_total = jnp.sum(weights, axis=1, keepdims=True)
        prob_low = (weights / row_total).astype(jnp.bfloat16)
        logsum = row_max[:, 0] + jnp.log(row_total[:, 0])
        return (unused, (matmul(prob_low, value_rows), logsum))

    head_ids = jnp.arange(query_heads.shape[0], dtype=jnp.int32)
    ignored, (head_outputs, logsum) = lax.scan(
        one_head, jnp.zeros((), jnp.float32), (query_heads, head_ids)
    )
    return (head_outputs, logsum)


def attend_back(query_heads, heads_of_key, heads_of_value, grad_heads, logsum, allowed, factor):
    heads_per_group = query_heads.shape[0] // heads_of_key.shape[0]

    def one_head(state, element):
        key_acc, value_acc = state
        query_rows, grad_rows, head_sum, head_index = element
        kv_index = head_index // heads_per_group
        key_rows = lax.dynamic_index_in_dim(heads_of_key, kv_index, 0, keepdims=False)
        value_rows = lax.dynamic_index_in_dim(heads_of_value, kv_index, 0, keepdims=False)
        scores = jnp.where(allowed, matmul_nt(query_rows, key_rows) * factor, NEG_FILL)
        probs = jnp.exp(scores - head_sum[:, None])
        prob_grad = matmul_nt(grad_rows, value_rows)
        score_grad = (
            probs * (prob_grad - jnp.sum(probs * prob_grad, axis=1, keepdims=True))
        ).astype(jnp.bfloat16)
        query_grad = matmul(score_grad, key_rows) * factor
        key_grad = matmul_tn(score_grad, query_rows) * factor
        value_grad = matmul_tn(probs.astype(jnp.bfloat16), grad_rows)
        key_acc = lax.dynamic_update_index_in_dim(
            key_acc,
            lax.dynamic_index_in_dim(key_acc, kv_index, 0, keepdims=False) + key_grad,
            kv_index,
            0,
        )
        value_acc = lax.dynamic_update_index_in_dim(
            value_acc,
            lax.dynamic_index_in_dim(value_acc, kv_index, 0, keepdims=False) + value_grad,
            kv_index,
            0,
        )
        return ((key_acc, value_acc), query_grad)

    head_ids = jnp.arange(query_heads.shape[0], dtype=jnp.int32)
    empty = jnp.zeros(heads_of_key.shape, jnp.float32)
    (key_acc, value_acc), query_grads = lax.scan(
        one_head, (empty, empty), (query_heads, grad_heads, logsum, head_ids)
    )
    return (query_grads, key_acc, value_acc)


def on_device(
    layer_input,
    norm1_gain,
    w_qkv,
    w_out,
    norm2_gain,
    w_gate,
    w_up,
    w_down,
    out_cotangent,
    seq_lengths,
    position_ids,
    deal_rows,
):
    own_rows, model_width = layer_input.shape
    row_devices = lax.axis_size("row")
    col_devices = lax.axis_size("col")
    block_rows = own_rows // row_devices
    rows_per_group = own_rows * col_devices
    row_ids = jnp.arange(row_devices, dtype=jnp.int32)
    targets = deal_rows[0]
    sender = jnp.sum(jnp.where(targets[:, None] == row_ids[None, :], row_ids[:, None], 0), axis=0)
    input_blocks = jnp.take(
        layer_input.reshape(row_devices, block_rows, model_width), sender, axis=0
    ).reshape(own_rows, model_width)
    cot_blocks = jnp.take(
        out_cotangent.reshape(row_devices, block_rows, model_width), sender, axis=0
    ).reshape(own_rows, model_width)
    dealt_input, dealt_cot = (
        lax.all_to_all(input_blocks, "row", split_axis=0, concat_axis=0, tiled=True),
        lax.all_to_all(cot_blocks, "row", split_axis=0, concat_axis=0, tiled=True),
    )
    qkv_mat, out_mat, gate_mat, up_mat, down_mat = (
        lax.all_gather(w_qkv, "row", axis=0, tiled=True),
        lax.all_gather(w_out, "row", axis=0, tiled=True),
        lax.all_gather(w_gate, "row", axis=0, tiled=True),
        lax.all_gather(w_up, "row", axis=0, tiled=True),
        lax.all_gather(w_down, "row", axis=0, tiled=True),
    )
    inputs_f = dealt_input.astype(jnp.float32)
    scale_one = rms_scale(inputs_f)
    normed_one = inputs_f * scale_one
    xn_one = (normed_one * norm1_gain).astype(jnp.bfloat16)
    xn_one_rows = gather_rows(xn_one)
    query_key_value_local = regroup_tokens(matmul(xn_one_rows, qkv_mat).astype(jnp.bfloat16))
    factor = 1.0 / math.sqrt(HEAD_DIMENSION)
    cosine_table, sine_table = rope_tables(position_ids, HEAD_DIMENSION)
    query_r = apply_rotation(
        query_key_value_local[:, :QUERY_FEATURES].astype(jnp.float32),
        cosine_table,
        sine_table,
        QUERY_HEADS,
    ).astype(jnp.bfloat16)
    key_repeated = apply_rotation(
        query_key_value_local[:, QUERY_FEATURES : QUERY_FEATURES + KEY_FEATURES].astype(
            jnp.float32
        ),
        cosine_table,
        sine_table,
        KEY_VALUE_HEADS,
    ).astype(jnp.bfloat16)
    value_own = query_key_value_local[:, QUERY_FEATURES + KEY_FEATURES :]
    key_full, value_full = (
        lax.all_gather(key_repeated, "col", axis=0, tiled=True),
        lax.all_gather(value_own, "col", axis=0, tiled=True),
    )
    col_index = lax.axis_index("col")
    key_ids = jnp.arange(rows_per_group, dtype=jnp.int32)
    query_ids = col_index * own_rows + jnp.arange(own_rows, dtype=jnp.int32)
    bounds = jnp.cumsum(seq_lengths[0])
    key_seg = jnp.sum((key_ids[:, None] >= bounds[None, :]).astype(jnp.int32), axis=1)
    query_seg = jnp.sum((query_ids[:, None] >= bounds[None, :]).astype(jnp.int32), axis=1)
    allowed = (query_seg[:, None] == key_seg[None, :]) & (key_ids[None, :] <= query_ids[:, None])
    query_heads = query_r.reshape(own_rows, QUERY_HEADS, HEAD_DIMENSION).transpose(1, 0, 2)
    heads_of_key = key_full.reshape(rows_per_group, KEY_VALUE_HEADS, HEAD_DIMENSION).transpose(
        1, 0, 2
    )
    heads_of_value = value_full.reshape(rows_per_group, KEY_VALUE_HEADS, HEAD_DIMENSION).transpose(
        1, 0, 2
    )
    head_outputs, logsum = attend(query_heads, heads_of_key, heads_of_value, allowed, factor)
    attn_own = (
        head_outputs.transpose(1, 0, 2).reshape(own_rows, QUERY_FEATURES).astype(jnp.bfloat16)
    )
    attn_cols = regroup_columns(attn_own)
    attn_proj = spread_sum(((attn_cols, out_mat),), own_rows)
    residual = inputs_f + attn_proj
    scale_two = rms_scale(residual)
    normed_two = residual * scale_two
    xn_two = (normed_two * norm2_gain).astype(jnp.bfloat16)
    xn_two_rows = gather_rows(xn_two)
    gate_pre = matmul(xn_two_rows, gate_mat)
    up_pre = matmul(xn_two_rows, up_mat)
    sigmoid_gate = jax.nn.sigmoid(gate_pre)
    hidden = (gate_pre * sigmoid_gate * up_pre).astype(jnp.bfloat16)
    mlp_proj = spread_sum(((hidden, down_mat),), own_rows)
    layer_out = (residual + mlp_proj).astype(jnp.bfloat16)
    cot_f = dealt_cot.astype(jnp.float32)
    cot_rows = gather_rows(dealt_cot)
    hidden_grad = matmul(cot_rows, down_mat)
    grad_down_part = matmul_tn(cot_rows, hidden)
    gate_grad = (
        hidden_grad * up_pre * sigmoid_gate * (1.0 + gate_pre * (1.0 - sigmoid_gate))
    ).astype(jnp.bfloat16)
    up_grad = (hidden_grad * gate_pre * sigmoid_gate).astype(jnp.bfloat16)
    xn_two_grad = spread_sum(((gate_grad, gate_mat), (up_grad, up_mat)), own_rows)
    grad_gate_part = matmul_tn(xn_two_rows, gate_grad)
    grad_up_part = matmul_tn(xn_two_rows, up_grad)
    gain_two_part = jnp.sum(xn_two_grad * normed_two, axis=0)
    normed_grad = xn_two_grad * norm2_gain
    residual_grad = cot_f + scale_two * (
        normed_grad - normed_two * jnp.mean(normed_grad * normed_two, axis=1, keepdims=True)
    )
    branch_grad = residual_grad.astype(jnp.bfloat16)
    branch_rows = gather_rows(branch_grad)
    attn_grad = regroup_tokens(matmul(branch_rows, out_mat).astype(jnp.bfloat16))
    grad_out_part = matmul_tn(branch_rows, attn_cols)
    grad_heads = attn_grad.reshape(own_rows, QUERY_HEADS, HEAD_DIMENSION).transpose(1, 0, 2)
    query_grads, key_acc, value_acc = attend_back(
        query_heads, heads_of_key, heads_of_value, grad_heads, logsum, allowed, factor
    )
    key_part = key_acc.transpose(1, 0, 2).reshape(rows_per_group, KEY_FEATURES)
    value_part = value_acc.transpose(1, 0, 2).reshape(rows_per_group, KEY_FEATURES)
    key_backward, value_back = (
        lax.psum_scatter(
            key_part.astype(jnp.bfloat16), "col", scatter_dimension=0, tiled=True
        ).astype(jnp.float32),
        lax.psum_scatter(
            value_part.astype(jnp.bfloat16), "col", scatter_dimension=0, tiled=True
        ).astype(jnp.float32),
    )
    query_back = reverse_rotation(
        query_grads.transpose(1, 0, 2).reshape(own_rows, QUERY_FEATURES),
        cosine_table,
        sine_table,
        QUERY_HEADS,
    )
    key_rotated = reverse_rotation(key_backward, cosine_table, sine_table, KEY_VALUE_HEADS)
    qkv_grad = jnp.concatenate([query_back, key_rotated, value_back], axis=1).astype(jnp.bfloat16)
    qkv_cols = regroup_columns(qkv_grad)
    xn_one_grad = spread_sum(((qkv_cols, qkv_mat),), own_rows)
    grad_qkv_part = matmul_tn(xn_one_rows, qkv_cols)
    gain_one_part = jnp.sum(xn_one_grad * normed_one, axis=0)
    normed_grad_one = xn_one_grad * norm1_gain
    input_grad = residual_grad + scale_one * (
        normed_grad_one - normed_one * jnp.mean(normed_grad_one * normed_one, axis=1, keepdims=True)
    )
    grad_qkv, grad_out, grad_gate, grad_up, grad_down = (
        lax.psum_scatter(grad_qkv_part, "row", scatter_dimension=0, tiled=True),
        lax.psum_scatter(grad_out_part, "row", scatter_dimension=0, tiled=True),
        lax.psum_scatter(grad_gate_part, "row", scatter_dimension=0, tiled=True),
        lax.psum_scatter(grad_up_part, "row", scatter_dimension=0, tiled=True),
        lax.psum_scatter(grad_down_part, "row", scatter_dimension=0, tiled=True),
    )
    grad_norm1, grad_norm2 = lax.psum((gain_one_part, gain_two_part), ("row", "col"))
    back_out, back_grad = (
        lax.all_to_all(layer_out, "row", split_axis=0, concat_axis=0, tiled=True),
        lax.all_to_all(
            input_grad.astype(jnp.bfloat16), "row", split_axis=0, concat_axis=0, tiled=True
        ),
    )
    layer_output = jnp.take(
        back_out.reshape(row_devices, block_rows, model_width), targets, axis=0
    ).reshape(own_rows, model_width)
    grad_input = jnp.take(
        back_grad.reshape(row_devices, block_rows, model_width), targets, axis=0
    ).reshape(own_rows, model_width)
    return (
        layer_output,
        grad_input,
        grad_norm1,
        grad_qkv,
        grad_out,
        grad_norm2,
        grad_gate,
        grad_up,
        grad_down,
    )


def solution(mesh):
    placed = (
        P(("row", "col"), None),
        P(),
        P("row", "col"),
        P("row", "col"),
        P(),
        P("row", "col"),
        P("row", "col"),
        P("row", "col"),
        P(("row", "col"), None),
        P("row", None),
        P(("row", "col")),
        P(("row", "col"), None),
    )
    return jax.shard_map(
        on_device,
        mesh=mesh,
        in_specs=placed,
        out_specs=(
            P(("row", "col"), None),
            P(("row", "col"), None),
            P(),
            P("row", "col"),
            P("row", "col"),
            P(),
            P("row", "col"),
            P("row", "col"),
            P("row", "col"),
        ),
        check_vma=False,
    )
```

profile of v0, /device:TPU:0, one launch (start us, length us, event | category | flops | bytes accessed | tf_op | source)
XLA Modules:
  0.0 1575.9 jit_solution(9520040302750912809)
XLA Ops:
  13.4 32.9 %all_to_all.100 = bf16[8,64,960]{2,1,0:T(8,128)(2,1)S(1)} all-to-all(bf16[8,64,960]{2,1,0:T(8,128)(2,1)S(1)} %get-tuple-element.545), channel_id=1, replica_groups=mesh['row'=8,'col'=4] {'row'}, dimensions={0} | all-to-all | bytes 1966080 | tf_op jit(solution)/shard_map/all_to_all | solution.py:194
  48.7 32.4 %all-gather = bf16[8,120,400]{1,2,0:T(8,128)(2,1)S(1)} all-gather(bf16[1,120,400]{1,2,0:T(8,128)(2,1)S(1)} %bitcast.267), channel_id=1, replica_groups=mesh['row'=8,'col'=4] {'row'}, dimensions={0}, use_global_device_ids=true | all-gather | bytes 864000 | tf_op jit(solution)/shard_map/all_gather | solution.py:198
  93.2 20.4 %all-to-all-done.1 = bf16[4,512,400]{1,2,0:T(8,128)(2,1)} async-done(((bf16[4,512,400]{1,2,0:T(8,128)(2,1)}), bf16[4,512,400]{1,2,0:T(8,128)(2,1)}, u32[]{:S(2)}, u32[]{:S(2)}) %all-to-all-start.1) | async-done | bytes 1638432 | tf_op jit(solution)/shard_map/all_to_all | solution.py:85
  122.2 10.6 all-gather.13.cloned.1.call-done
  136.6 16.6 %all-gather.15.cloned.1.call-done = bf16[2048,320]{0,1:T(8,128)(2,1)} async-done(((bf16[512,320]{0,1:T(8,128)(2,1)}), bf16[2048,320]{0,1:T(8,128)(2,1)}) %all-gather.15.cloned.1.call-update) | async-done | bytes 1310736 | tf_op jit(solution)/shard_map/all_gather | solution.py:229
  156.9 146.1 %while.34 = (s32[]{:T(128)}, bf16[15,512,64]{1,2,0:T(8,128)(2,1)}, f32[15,512]{1,0:T(8,128)}, bf16[15,512,64]{2,1,0:T(8,128)(2,1)}, s32[15]{0:T(128)S(1)}, /*ind...) while((s32[]{:T(128)}, bf16[15,512,64]{1,2,0:T(8,128)(2,1)}, ...), condition=%wide.region_8.10_spmd.clone.clone, body=%wide.region_5.9_spmd.clone.sunk.clone | while | flops 279969280 | bytes 13926677 | solution.py:119
  306.6 31.5 %all_gather.37 = bf16[960,240]{1,0:T(8,128)(2,1)S(1)} all-gather(bf16[120,240]{1,0:T(8,128)(2,1)S(1)} %copy-done.24), channel_id=1, replica_groups=mesh['row'=8,'col'=4] {'row'}, dimensions={0}, use_global_device_ids=true | all-gather | bytes 518400 | tf_op jit(solution)/shard_map/all_gather | solution.py:199
  344.3 69.5 %reduce-scatter.20.cloned.1.call-done = f32[512,960]{0,1:T(8,128)} async-done(((f32[2048,960]{0,1:T(8,128)}), f32[512,960]{0,1:T(8,128)}) %reduce-scatter.20.cloned.1.call-update) | async-done | bytes 1966096 | tf_op jit(solution)/shard_map/reduce_scatter | solution.py:96
  419.7 31.2 %all_to_all.101 = bf16[8,64,960]{2,1,0:T(8,128)(2,1)} all-to-all(bf16[8,64,960]{2,1,0:T(8,128)(2,1)S(1)} %copy-done.8), channel_id=1, replica_groups=mesh['row'=8,'col'=4] {'row'}, dimensions={0} | all-to-all | bytes 1966080 | tf_op jit(solution)/shard_map/all_to_all | solution.py:195
  451.3 8.3 fusion.50
  459.6 35.7 %all-gather.19.cloned.1.call-done = bf16[960,640]{1,0:T(8,128)(2,1)} async-done(((bf16[120,640]{1,0:T(8,128)(2,1)}), bf16[960,640]{1,0:T(8,128)(2,1)}) %all-gather.19.cloned.1.call-update) | async-done | bytes 1228816 | tf_op jit(solution)/shard_map/all_gather | solution.py:200
  495.3 8.3 fusion.49
  503.6 34.6 %all-gather.23.cloned.1.call-done = bf16[960,640]{1,0:T(8,128)(2,1)} async-done(((bf16[120,640]{1,0:T(8,128)(2,1)}), bf16[960,640]{1,0:T(8,128)(2,1)}) %all-gather.23.cloned.1.call-update) | async-done | bytes 1228816 | tf_op jit(solution)/shard_map/all_gather | solution.py:202
  538.2 34.7 %all-gather.25.cloned.1.call-done = bf16[2048,960]{1,0:T(8,128)(2,1)} async-done(((bf16[512,960]{1,0:T(8,128)(2,1)}), bf16[2048,960]{1,0:T(8,128)(2,1)}) %all-gather.25.cloned.1.call-update) | async-done | bytes 3932176 | tf_op jit(solution)/shard_map/all_gather | solution.py:81
  572.9 10.5 multiply_convert_fusion.1
  594.6 66.5 %reduce-scatter.24.cloned.1.call-done = f32[512,960]{0,1:T(8,128)} async-done(((f32[2048,960]{0,1:T(8,128)}), f32[512,960]{0,1:T(8,128)}) %reduce-scatter.24.cloned.1.call-update) | async-done | bytes 1966096 | tf_op jit(solution)/shard_map/reduce_scatter | solution.py:96
  664.9 33.2 %all-gather.27.cloned.1.call-done = bf16[2048,960]{0,1:T(8,128)(2,1)} async-done(((bf16[512,960]{0,1:T(8,128)(2,1)}), bf16[2048,960]{0,1:T(8,128)(2,1)}) %all-gather.27.cloned.1.call-update) | async-done | bytes 3932176 | tf_op jit(solution)/shard_map/all_gather | solution.py:81
  706.0 13.7 all-to-all-done.5
  722.7 236.6 %while.35 = (s32[]{:T(128)}, f32[5,2048,64]{1,2,0:T(8,128)}, f32[5,2048,64]{1,2,0:T(8,128)S(1)}, f32[15,512,64]{1,2,0:T(8,128)}, s32[15]{0:T(128)S(1)}, /*index=...) while((s32[]{:T(128)}, f32[5,2048,64]{1,2,0:T(8,128)}, ...), condition=%wide.region_16.18_spmd.clone.clone, body=%wide.region_14.17_spmd.clone.sunk.clone | while | flops 684097024 | bytes 37771592 | solution.py:159
  965.7 23.3 %reduce-scatter.26.cloned.1.call-done = bf16[512,320]{0,1:T(8,128)(2,1)} async-done(((bf16[2048,320]{0,1:T(8,128)(2,1)}), bf16[512,320]{0,1:T(8,128)(2,1)}) %reduce-scatter.26.cloned.1.call-update) | async-done | bytes 327696 | tf_op jit(solution)/shard_map/reduce_scatter | solution.py:289
  990.2 28.1 %reduce-scatter.28.cloned.1.call-done = bf16[512,320]{0,1:T(8,128)(2,1)} async-done(((bf16[2048,320]{0,1:T(8,128)(2,1)}), bf16[512,320]{0,1:T(8,128)(2,1)}) %reduce-scatter.28.cloned.1.call-update) | async-done | bytes 327696 | tf_op jit(solution)/shard_map/reduce_scatter | solution.py:292
  1019.4 23.3 %all_to_all.102 = bf16[512,4,400]{0,2,1:T(8,128)(2,1)S(1)} all-to-all(bf16[512,4,400]{0,2,1:T(8,128)(2,1)S(1)} %bitcast.241), channel_id=1, replica_groups=mesh['row'=8,'col'=4] {'col'}, dimensions={1} | all-to-all | bytes 3276800 | tf_op jit(solution)/shard_map/all_to_all | solution.py:89
  1064.4 7.9 fusion.58
  1087.2 30.1 %reduce-scatter.30.cloned.1.call-done = f32[512,960]{0,1:T(8,128)} async-done(((f32[2048,960]{0,1:T(8,128)}), f32[512,960]{0,1:T(8,128)}) %reduce-scatter.30.cloned.1.call-update) | async-done | bytes 1966096 | tf_op jit(solution)/shard_map/reduce_scatter | solution.py:96
  1119.5 69.3 %reduce-scatter.22.cloned.1.call-done = f32[512,960]{0,1:T(8,128)} async-done(((f32[2048,960]{0,1:T(8,128)}), f32[512,960]{0,1:T(8,128)}) %reduce-scatter.22.cloned.1.call-update) | async-done | bytes 1966096 | tf_op jit(solution)/shard_map/reduce_scatter | solution.py:96
  1202.9 38.0 %all-to-all-done.7 = bf16[8,64,960]{2,1,0:T(8,128)(2,1)S(1)} async-done(((bf16[8,64,960]{2,1,0:T(8,128)(2,1)}), bf16[8,64,960]{2,1,0:T(8,128)(2,1)S(1)}, u32[]{:S(2)}, u32[]{:S(2)}) %all-to-all-start.7) | async-done | bytes 983072 | tf_op jit(solution)/shard_map/all_to_all | solution.py:322
  1248.9 31.4 %reduce-scatter.34.cloned.1.call-done = f32[120,400]{1,0:T(8,128)} async-done(((f32[960,400]{1,0:T(8,128)}), f32[120,400]{1,0:T(8,128)}) %reduce-scatter.34.cloned.1.call-update) | async-done | bytes 192016
  1282.1 39.7 %all-reduce.3 = (f32[960]{0:T(1024)}, f32[960]{0:T(1024)}) all-reduce(f32[960]{0:T(1024)S(1)} %get-tuple-element.467, f32[960]{0:T(1024)S(1)} %get-tuple-element.465), channel_id=1, replica_groups=mesh['row'=8,'col'=4] {'row','col'}, use_global_device_ids=true, to_apply=%region_22.24 | all-reduce | flops 1920 | bytes 15360 | tf_op jit(solution)/shard_map/psum | solution.py:319
  1327.9 26.9 %reduce-scatter.40.cloned.1.call-done = f32[120,640]{1,0:T(8,128)} async-done(((f32[960,640]{1,0:T(8,128)}), f32[120,640]{1,0:T(8,128)}) %reduce-scatter.40.cloned.1.call-update) | async-done | bytes 307216
  1354.8 73.3 %reduce-scatter.36.cloned.1.call-done = f32[120,640]{1,0:T(8,128)} async-done(((f32[960,640]{1,0:T(8,128)}), f32[120,640]{1,0:T(8,128)}) %reduce-scatter.36.cloned.1.call-update) | async-done | bytes 307216
  1428.1 73.4 %reduce-scatter.38.cloned.1.call-done = f32[120,640]{1,0:T(8,128)} async-done(((f32[960,640]{1,0:T(8,128)}), f32[120,640]{1,0:T(8,128)}) %reduce-scatter.38.cloned.1.call-update) | async-done | bytes 307216
  1501.5 66.6 %reduce-scatter.32.cloned.1.call-done = f32[120,240]{1,0:T(8,128)} async-done(((f32[960,240]{1,0:T(8,128)}), f32[120,240]{1,0:T(8,128)}) %reduce-scatter.32.cloned.1.call-update) | async-done | bytes 115216 | tf_op jit(solution)/shard_map/reduce_scatter | solution.py:314
  (430 shorter events, 477.3 us)
Async XLA Ops:
  8.0 74.8 %all-gather.11.cloned.1.call-start = ((), (), s32[]{:S(2)}) async-start(), calls=%async_computation.19 | async-start | bytes 4915200 | tf_op jit(solution)/shard_map/all_gather | solution.py:81
  47.3 366.5 %copy-start = (f32[512,960]{0,1:T(8,128)}, f32[512,960]{0,1:T(8,128)S(1)}, u32[]{:S(2)}) copy-start(f32[512,960]{0,1:T(8,128)S(1)} %copy.93) | copy-start | bytes 5898244
  88.4 25.2 %all-to-all-start.1 = ((bf16[4,512,400]{1,2,0:T(8,128)(2,1)}), bf16[4,512,400]{1,2,0:T(8,128)(2,1)}, u32[]{:S(2)}, u32[]{:S(2)}) async-start(bf16[4,512,400]{1,2,0:T(8,128)(2,1)} %bitcast.240), calls=%async_computation.1 | async-start | bytes 3276800 | tf_op jit(solution)/shard_map/all_to_all | solution.py:85
  92.7 40.0 %all-gather.13.cloned.1.call-start = ((), (), s32[]{:S(2)}) async-start(), calls=%async_computation.20 | async-start | bytes 1638400 | tf_op jit(solution)/shard_map/all_gather | solution.py:228
  116.4 36.8 %all-gather.15.cloned.1.call-start = ((), (), s32[]{:S(2)}) async-start(), calls=%async_computation.21 | async-start | bytes 1638400 | tf_op jit(solution)/shard_map/all_gather | solution.py:229
  156.9 149.7 %copy-start.24 = (bf16[120,240]{1,0:T(8,128)(2,1)S(1)}, bf16[120,240]{1,0:T(8,128)(2,1)}, u32[]{:S(2)}) copy-start(bf16[120,240]{1,0:T(8,128)(2,1)} %param.21) | copy-start | bytes 172804
  303.0 35.1 %all-to-all-start.2 = ((bf16[512,4,240]{0,2,1:T(8,128)(2,1)}), bf16[512,4,240]{0,2,1:T(8,128)(2,1)S(1)}, u32[]{:S(2)}, u32[]{:S(2)}) async-start(bf16[512,4,240]{0,2,1:T(8,128)(2,1)} %bitcast.20), calls=%async_computation.2 | async-start | bytes 1966080 | tf_op jit(solution)/shard_map/all_to_all | solution.py:89
  306.5 107.3 %reduce-scatter.20.cloned.1.call-start = ((), (), s32[]{:S(2)}) async-start(), calls=%async_computation.22 | async-start | bytes 9830400 | tf_op jit(solution)/shard_map/reduce_scatter | solution.py:96
  343.4 107.5 %all-gather.21.cloned.1.call-start = ((), (), s32[]{:S(2)}) async-start(), calls=%async_computation.25 | async-start | bytes 1382400 | tf_op jit(solution)/shard_map/all_gather | solution.py:201
  344.0 73.1 %copy-start.23 = (f32[960]{0:T(1024)S(1)}, f32[960]{0:T(1024)}, u32[]{:S(2)}) copy-start(f32[960]{0:T(1024)} %param.22) | copy-start | bytes 11524
  344.0 107.2 %all-gather.17.cloned.1.call-start = ((), (), s32[]{:S(2)}) async-start(), calls=%async_computation.23 | async-start | bytes 4915200 | tf_op jit(solution)/shard_map/all_gather | solution.py:81
  418.3 76.9 %all-gather.19.cloned.1.call-start = ((), (), s32[]{:S(2)}) async-start(), calls=%async_computation.24 | async-start | bytes 1382400 | tf_op jit(solution)/shard_map/all_gather | solution.py:200
  418.9 119.2 %all-gather.23.cloned.1.call-start = ((), (), s32[]{:S(2)}) async-start(), calls=%async_computation.26 | async-start | bytes 1382400 | tf_op jit(solution)/shard_map/all_gather | solution.py:202
  419.7 153.2 %all-gather.25.cloned.1.call-start = ((), (), s32[]{:S(2)}) async-start(), calls=%async_computation.28 | async-start | bytes 5242880 | tf_op jit(solution)/shard_map/all_gather | solution.py:81
  450.9 210.2 %reduce-scatter.24.cloned.1.call-start = ((), (), s32[]{:S(2)}) async-start(), calls=%async_computation.29 | async-start | bytes 9830400 | tf_op jit(solution)/shard_map/reduce_scatter | solution.py:96
  503.6 79.8 %copy-start.31 = (bf16[960,640]{1,0:T(8,128)(2,1)S(1)}, bf16[960,640]{1,0:T(8,128)(2,1)}, u32[]{:S(2)}) copy-start(bf16[960,640]{1,0:T(8,128)(2,1)} %all-gather.19.cloned.1.call-done) | copy-start | bytes 3686404
  592.1 69.0 %copy-start.3 = (f32[512,960]{0,1:T(8,128)S(1)}, f32[512,960]{0,1:T(8,128)}, u32[]{:S(2)}) copy-start(f32[512,960]{0,1:T(8,128)} %copy-done.2) | copy-start | bytes 5898244
  592.1 106.0 %all-gather.27.cloned.1.call-start = ((), (), s32[]{:S(2)}) async-start(), calls=%async_computation.30 | async-start | bytes 4915200 | tf_op jit(solution)/shard_map/all_gather | solution.py:81
  594.6 68.8 %copy-start.6 = (bf16[512,960]{0,1:T(8,128)(2,1)S(1)}, bf16[512,960]{0,1:T(8,128)(2,1)}, u32[]{:S(2)}) copy-start(bf16[512,960]{0,1:T(8,128)(2,1)} %copy.96) | copy-start | bytes 2949124
  702.4 17.2 %all-to-all-start.5 = ((bf16[4,512,240]{1,2,0:T(8,128)(2,1)}), bf16[4,512,240]{1,2,0:T(8,128)(2,1)S(1)}, u32[]{:S(2)}, u32[]{:S(2)}) async-start(bf16[4,512,240]{1,2,0:T(8,128)(2,1)} %bitcast.164), calls=%async_computation.8 | async-start | bytes 1966080 | tf_op jit(solution)/shard_map/all_to_all | solution.py:85
  705.9 283.1 %reduce-scatter.26.cloned.1.call-start = ((), (), s32[]{:S(2)}) async-start(), calls=%async_computation.31 | async-start | bytes 1638400 | tf_op jit(solution)/shard_map/reduce_scatter | solution.py:289
  962.3 56.0 %reduce-scatter.28.cloned.1.call-start = ((), (), s32[]{:S(2)}) async-start(), calls=%async_computation.32 | async-start | bytes 1638400 | tf_op jit(solution)/shard_map/reduce_scatter | solution.py:292
  963.7 153.6 %reduce-scatter.30.cloned.1.call-start = ((), (), s32[]{:S(2)}) async-start(), calls=%async_computation.33 | async-start | bytes 9830400 | tf_op jit(solution)/shard_map/reduce_scatter | solution.py:96
  1048.4 140.5 %reduce-scatter.22.cloned.1.call-start = ((), (), s32[]{:S(2)}) async-start(), calls=%async_computation.27 | async-start | bytes 9830400 | tf_op jit(solution)/shard_map/reduce_scatter | solution.py:96
  1057.5 222.8 %reduce-scatter.34.cloned.1.call-start = ((), (), s32[]{:S(2)}) async-start(), calls=%async_computation.35 | async-start | bytes 2211840
  1064.2 290.7 %reduce-scatter.40.cloned.1.call-start = ((), (), s32[]{:S(2)}) async-start(), calls=%async_computation.38 | async-start | bytes 2764800
  1072.3 355.8 %reduce-scatter.36.cloned.1.call-start = ((), (), s32[]{:S(2)}) async-start(), calls=%async_computation.36 | async-start | bytes 2764800
  1080.4 421.2 %reduce-scatter.38.cloned.1.call-start = ((), (), s32[]{:S(2)}) async-start(), calls=%async_computation.37 | async-start | bytes 2764800
  1087.2 101.6 %copy-start.7 = (bf16[512,960]{0,1:T(8,128)(2,1)S(1)}, bf16[512,960]{0,1:T(8,128)(2,1)}, u32[]{:S(2)}) copy-start(bf16[512,960]{0,1:T(8,128)(2,1)} %copy.96) | copy-start | bytes 2949124
  1195.9 44.9 %all-to-all-start.7 = ((bf16[8,64,960]{2,1,0:T(8,128)(2,1)}), bf16[8,64,960]{2,1,0:T(8,128)(2,1)S(1)}, u32[]{:S(2)}, u32[]{:S(2)}) async-start(bf16[8,64,960]{2,1,0:T(8,128)(2,1)} %bitcast.42), calls=%async_computation.13 | async-start | bytes 2097152 | tf_op jit(solution)/shard_map/all_to_all | solution.py:322
  1240.8 81.6 %all-to-all-start.3 = ((bf16[8,64,960]{2,1,0:T(8,128)(2,1)}), bf16[8,64,960]{2,1,0:T(8,128)(2,1)S(1)}, u32[]{:S(2)}, u32[]{:S(2)}) async-start(bf16[8,64,960]{2,1,0:T(8,128)(2,1)} %bitcast.22), calls=%async_computation.5 | async-start | bytes 2097152 | tf_op jit(solution)/shard_map/all_to_all | solution.py:321
  1244.4 323.7 %reduce-scatter.32.cloned.1.call-start = ((), (), s32[]{:S(2)}) async-start(), calls=%async_computation.34 | async-start | bytes 1105920 | tf_op jit(solution)/shard_map/reduce_scatter | solution.py:314
  (28 other events, 345.0 us)
Sparse Core Ops, SparseCore 0:
  48.8 32.0 all-gather.10
  116.5 16.2 all-gather.12
  134.9 18.1 all-gather.14
  343.6 70.1 reduce-scatter.19
  665.0 32.9 all-gather.26
  962.5 26.5 reduce-scatter.25
  991.7 26.5 reduce-scatter.27
Sparse Core Ops, SparseCore 1:
  346.1 42.9 all-gather.20
  418.4 32.8 all-gather.16
  453.6 41.7 all-gather.18
  497.7 40.4 all-gather.22
  539.8 33.0 all-gather.24
  592.2 68.8 reduce-scatter.23
  1048.4 68.9 reduce-scatter.29
  1119.9 68.8 reduce-scatter.21
  1192.2 88.1 reduce-scatter.33
  1285.0 69.8 reduce-scatter.39
  1359.3 68.7 reduce-scatter.35
  1432.8 68.7 reduce-scatter.37
  1505.7 62.3 reduce-scatter.31
where the time goes:
time: 1590 us; the launch traced here: 1580 us
  waiting for transfers between devices  799 us (50%)
  matrix products  335 us (21%)
  blocking collectives  191 us (12%)
  local copies, waits for them, and re-layouts  105 us (7%)
  loops' own time  59.9 us (4%)
  other arithmetic  47.7 us (3%)
  starting transfers between devices  21.8 us (1%)
  between operations  16.8 us (1%)
    reduce_scatter x4, waiting for transfers between devices, spread_sum(): return lax.psum_scatter(result, 'col', scatter_dimension=0, tiled=True)  235 us
    unnamed x24, waiting for transfers between devices  208 us
    dot_general x50, matrix products, matmul_nt(): lax.dot_general(left_mat, right_mat, (((1,), (1,)), ((), ())), preferred_...  134 us
    dot_general x35, matrix products, matmul(): return jnp.dot(left_mat, right_mat, preferred_element_type=jnp.float32)  113 us
    dot_general x34, matrix products, matmul_tn(): lax.dot_general(left_mat, right_mat, (((0,), (0,)), ((), ())), preferred_...  80.8 us
    all_gather x4, waiting for transfers between devices, gather_rows(): return lax.all_gather(values, 'col', axis=0, tiled=True)  68.1 us
    reduce_scatter x1, waiting for transfers between devices, on_device(): lax.psum_scatter(grad_out_part, 'row', scatter_dimension=0, tiled=True)  66.6 us
    psum x1, blocking collectives, on_device(): lax.psum((gain_one_part, gain_two_part), ('row', 'col'))  39.7 us
  transfers between devices with their start and end apart: 25, of which 21 were waited for; matrix products, arithmetic and copies ran while one was open for 6% of the time, Pallas kernels for 0%

commit v1 on v0

--- a/solution.py
+++ b/solution.py
@@ -12,6 +12,12 @@
 EPS = 1e-05
 NEG_FILL = -1e30
 THETA = 10000.0
+
+
+def render_slices_by_axis(tile_in, mesh_name, peer_axis):
+    for d in (mesh_name, peer_axis):
+        tile_in = lax.psum(tile_in, axis_name=d)
+    return tile_in
 
 
 def matmul(left_mat, right_mat):
@@ -316,7 +322,7 @@
         lax.psum_scatter(grad_up_part, "row", scatter_dimension=0, tiled=True),
         lax.psum_scatter(grad_down_part, "row", scatter_dimension=0, tiled=True),
     )
-    grad_norm1, grad_norm2 = lax.psum((gain_one_part, gain_two_part), ("row", "col"))
+    grad_norm1, grad_norm2 = render_slices_by_axis((gain_one_part, gain_two_part), "col", "row")
     back_out, back_grad = (
         lax.all_to_all(layer_out, "row", split_axis=0, concat_axis=0, tiled=True),
         lax.all_to_all(

time: 1590 us -> 1590 us (level)
    psum x1 -> x2, blocking collectives: 39.7 us -> 26.4 us  [render_slices_by_axis(): tile_in = lax.psum(tile_in, axis_name=d)]
where the time goes in v1:
time: 1590 us; the launch traced here: 1580 us
  waiting for transfers between devices  812 us (51%)
  matrix products  335 us (21%)
  blocking collectives  178 us (11%)
  local copies, waits for them, and re-layouts  105 us (7%)
  loops' own time  59.9 us (4%)
  other arithmetic  47.8 us (3%)
  starting transfers between devices  21.8 us (1%)
  between operations  16.8 us (1%)
    reduce_scatter x4, waiting for transfers between devices, spread_sum(): return lax.psum_scatter(result, 'col', scatter_dimension=0, tiled=True)  235 us
    unnamed x24, waiting for transfers between devices  221 us
    dot_general x50, matrix products, matmul_nt(): lax.dot_general(left_mat, right_mat, (((1,), (1,)), ((), ())), preferred_...  134 us
    dot_general x35, matrix products, matmul(): return jnp.dot(left_mat, right_mat, preferred_element_type=jnp.float32)  113 us
    dot_general x34, matrix products, matmul_tn(): lax.dot_general(left_mat, right_mat, (((0,), (0,)), ((), ())), preferred_...  80.8 us
    all_gather x4, waiting for transfers between devices, gather_rows(): return lax.all_gather(values, 'col', axis=0, tiled=True)  68.1 us
    reduce_scatter x1, waiting for transfers between devices, on_device(): lax.psum_scatter(grad_out_part, 'row', scatter_dimension=0, tiled=True)  66.6 us
    all_to_all x1, waiting for transfers between devices, on_device(): lax.all_to_all(input_grad.astype(jnp.bfloat16), 'row', split_axis=0, conc...  38 us
  transfers between devices with their start and end apart: 25, of which 21 were waited for; matrix products, arithmetic and copies ran while one was open for 6% of the time, Pallas kernels for 0%

profile of v1, /device:TPU:0, one launch (start us, length us, event | category | flops | bytes accessed | tf_op | source)
XLA Modules:
  0.0 1575.9 jit_solution(9671384849987366876)
XLA Ops:
  13.4 32.9 %all_to_all.100 = bf16[8,64,960]{2,1,0:T(8,128)(2,1)S(1)} all-to-all(bf16[8,64,960]{2,1,0:T(8,128)(2,1)S(1)} %get-tuple-element.547), channel_id=1, replica_groups=mesh['row'=8,'col'=4] {'row'}, dimensions={0} | all-to-all | bytes 1966080 | tf_op jit(solution)/shard_map/all_to_all | solution.py:200
  48.7 32.4 %all-gather = bf16[8,120,400]{1,2,0:T(8,128)(2,1)S(1)} all-gather(bf16[1,120,400]{1,2,0:T(8,128)(2,1)S(1)} %bitcast.267), channel_id=1, replica_groups=mesh['row'=8,'col'=4] {'row'}, dimensions={0}, use_global_device_ids=true | all-gather | bytes 864000 | tf_op jit(solution)/shard_map/all_gather | solution.py:204
  93.2 20.4 %all-to-all-done.1 = bf16[4,512,400]{1,2,0:T(8,128)(2,1)} async-done(((bf16[4,512,400]{1,2,0:T(8,128)(2,1)}), bf16[4,512,400]{1,2,0:T(8,128)(2,1)}, u32[]{:S(2)}, u32[]{:S(2)}) %all-to-all-start.1) | async-done | bytes 1638432 | tf_op jit(solution)/shard_map/all_to_all | solution.py:91
  122.3 10.5 all-gather.13.cloned.1.call-done
  136.6 16.6 %all-gather.15.cloned.1.call-done = bf16[2048,320]{0,1:T(8,128)(2,1)} async-done(((bf16[512,320]{0,1:T(8,128)(2,1)}), bf16[2048,320]{0,1:T(8,128)(2,1)}) %all-gather.15.cloned.1.call-update) | async-done | bytes 1310736 | tf_op jit(solution)/shard_map/all_gather | solution.py:235
  157.0 146.1 %while.34 = (s32[]{:T(128)}, bf16[15,512,64]{1,2,0:T(8,128)(2,1)}, f32[15,512]{1,0:T(8,128)}, bf16[15,512,64]{2,1,0:T(8,128)(2,1)}, s32[15]{0:T(128)S(1)}, /*ind...) while((s32[]{:T(128)}, bf16[15,512,64]{1,2,0:T(8,128)(2,1)}, ...), condition=%wide.region_8.10_spmd.clone.clone, body=%wide.region_5.9_spmd.clone.sunk.clone | while | flops 279969280 | bytes 13926677 | solution.py:125
  306.6 31.5 %all_gather.37 = bf16[960,240]{1,0:T(8,128)(2,1)S(1)} all-gather(bf16[120,240]{1,0:T(8,128)(2,1)S(1)} %copy-done.24), channel_id=1, replica_groups=mesh['row'=8,'col'=4] {'row'}, dimensions={0}, use_global_device_ids=true | all-gather | bytes 518400 | tf_op jit(solution)/shard_map/all_gather | solution.py:205
  344.3 69.5 %reduce-scatter.20.cloned.1.call-done = f32[512,960]{0,1:T(8,128)} async-done(((f32[2048,960]{0,1:T(8,128)}), f32[512,960]{0,1:T(8,128)}) %reduce-scatter.20.cloned.1.call-update) | async-done | bytes 1966096 | tf_op jit(solution)/shard_map/reduce_scatter | solution.py:102
  419.8 31.2 %all_to_all.101 = bf16[8,64,960]{2,1,0:T(8,128)(2,1)} all-to-all(bf16[8,64,960]{2,1,0:T(8,128)(2,1)S(1)} %copy-done.8), channel_id=1, replica_groups=mesh['row'=8,'col'=4] {'row'}, dimensions={0} | all-to-all | bytes 1966080 | tf_op jit(solution)/shard_map/all_to_all | solution.py:201
  451.3 8.3 fusion.50
  459.6 35.7 %all-gather.19.cloned.1.call-done = bf16[960,640]{1,0:T(8,128)(2,1)} async-done(((bf16[120,640]{1,0:T(8,128)(2,1)}), bf16[960,640]{1,0:T(8,128)(2,1)}) %all-gather.19.cloned.1.call-update) | async-done | bytes 1228816 | tf_op jit(solution)/shard_map/all_gather | solution.py:206
  495.3 8.3 fusion.49
  503.6 34.6 %all-gather.23.cloned.1.call-done = bf16[960,640]{1,0:T(8,128)(2,1)} async-done(((bf16[120,640]{1,0:T(8,128)(2,1)}), bf16[960,640]{1,0:T(8,128)(2,1)}) %all-gather.23.cloned.1.call-update) | async-done | bytes 1228816 | tf_op jit(solution)/shard_map/all_gather | solution.py:208
  538.2 34.7 %all-gather.25.cloned.1.call-done = bf16[2048,960]{1,0:T(8,128)(2,1)} async-done(((bf16[512,960]{1,0:T(8,128)(2,1)}), bf16[2048,960]{1,0:T(8,128)(2,1)}) %all-gather.25.cloned.1.call-update) | async-done | bytes 3932176 | tf_op jit(solution)/shard_map/all_gather | solution.py:87
  572.9 10.5 multiply_convert_fusion.1
  594.6 66.5 %reduce-scatter.24.cloned.1.call-done = f32[512,960]{0,1:T(8,128)} async-done(((f32[2048,960]{0,1:T(8,128)}), f32[512,960]{0,1:T(8,128)}) %reduce-scatter.24.cloned.1.call-update) | async-done | bytes 1966096 | tf_op jit(solution)/shard_map/reduce_scatter | solution.py:102
  664.9 33.2 %all-gather.27.cloned.1.call-done = bf16[2048,960]{0,1:T(8,128)(2,1)} async-done(((bf16[512,960]{0,1:T(8,128)(2,1)}), bf16[2048,960]{0,1:T(8,128)(2,1)}) %all-gather.27.cloned.1.call-update) | async-done | bytes 3932176 | tf_op jit(solution)/shard_map/all_gather | solution.py:87
  706.0 13.7 all-to-all-done.5
  722.7 236.5 %while.35 = (s32[]{:T(128)}, f32[5,2048,64]{1,2,0:T(8,128)}, f32[5,2048,64]{1,2,0:T(8,128)S(1)}, f32[15,512,64]{1,2,0:T(8,128)}, s32[15]{0:T(128)S(1)}, /*index=...) while((s32[]{:T(128)}, f32[5,2048,64]{1,2,0:T(8,128)}, ...), condition=%wide.region_16.18_spmd.clone.clone, body=%wide.region_14.17_spmd.clone.sunk.clone | while | flops 684097024 | bytes 37771592 | solution.py:165
  965.7 23.3 %reduce-scatter.26.cloned.1.call-done = bf16[512,320]{0,1:T(8,128)(2,1)} async-done(((bf16[2048,320]{0,1:T(8,128)(2,1)}), bf16[512,320]{0,1:T(8,128)(2,1)}) %reduce-scatter.26.cloned.1.call-update) | async-done | bytes 327696 | tf_op jit(solution)/shard_map/reduce_scatter | solution.py:295
  990.1 28.1 %reduce-scatter.28.cloned.1.call-done = bf16[512,320]{0,1:T(8,128)(2,1)} async-done(((bf16[2048,320]{0,1:T(8,128)(2,1)}), bf16[512,320]{0,1:T(8,128)(2,1)}) %reduce-scatter.28.cloned.1.call-update) | async-done | bytes 327696 | tf_op jit(solution)/shard_map/reduce_scatter | solution.py:298
  1019.3 23.3 %all_to_all.102 = bf16[512,4,400]{0,2,1:T(8,128)(2,1)S(1)} all-to-all(bf16[512,4,400]{0,2,1:T(8,128)(2,1)S(1)} %bitcast.241), channel_id=1, replica_groups=mesh['row'=8,'col'=4] {'col'}, dimensions={1} | all-to-all | bytes 3276800 | tf_op jit(solution)/shard_map/all_to_all | solution.py:95
  1064.3 7.9 fusion.58
  1087.1 30.1 %reduce-scatter.30.cloned.1.call-done = f32[512,960]{0,1:T(8,128)} async-done(((f32[2048,960]{0,1:T(8,128)}), f32[512,960]{0,1:T(8,128)}) %reduce-scatter.30.cloned.1.call-update) | async-done | bytes 1966096 | tf_op jit(solution)/shard_map/reduce_scatter | solution.py:102
  1119.4 69.3 %reduce-scatter.22.cloned.1.call-done = f32[512,960]{0,1:T(8,128)} async-done(((f32[2048,960]{0,1:T(8,128)}), f32[512,960]{0,1:T(8,128)}) %reduce-scatter.22.cloned.1.call-update) | async-done | bytes 1966096 | tf_op jit(solution)/shard_map/reduce_scatter | solution.py:102
  1202.8 38.0 %all-to-all-done.7 = bf16[8,64,960]{2,1,0:T(8,128)(2,1)S(1)} async-done(((bf16[8,64,960]{2,1,0:T(8,128)(2,1)}), bf16[8,64,960]{2,1,0:T(8,128)(2,1)S(1)}, u32[]{:S(2)}, u32[]{:S(2)}) %all-to-all-start.7) | async-done | bytes 983072 | tf_op jit(solution)/shard_map/all_to_all | solution.py:328
  1248.8 31.4 %reduce-scatter.34.cloned.1.call-done = f32[120,400]{1,0:T(8,128)} async-done(((f32[960,400]{1,0:T(8,128)}), f32[120,400]{1,0:T(8,128)}) %reduce-scatter.34.cloned.1.call-update) | async-done | bytes 192016
  1287.7 20.7 %all-reduce.3 = (f32[960]{0:T(1024)}, f32[960]{0:T(1024)}) all-reduce(f32[960]{0:T(1024)S(1)} %get-tuple-element.517, f32[960]{0:T(1024)S(1)} %get-tuple-element.518), channel_id=1, replica_groups=mesh['row'=8,'col'=4] {'row'}, use_global_device_ids=true, to_apply=%region_23.25 | all-reduce | flops 1920 | bytes 15360 | tf_op jit(solution)/shard_map/psum | solution.py:19
  1314.5 39.5 %reduce-scatter.40.cloned.1.call-done = f32[120,640]{1,0:T(8,128)} async-done(((f32[960,640]{1,0:T(8,128)}), f32[120,640]{1,0:T(8,128)}) %reduce-scatter.40.cloned.1.call-update) | async-done | bytes 307216
  1353.9 73.7 %reduce-scatter.36.cloned.1.call-done = f32[120,640]{1,0:T(8,128)} async-done(((f32[960,640]{1,0:T(8,128)}), f32[120,640]{1,0:T(8,128)}) %reduce-scatter.36.cloned.1.call-update) | async-done | bytes 307216
  1427.7 73.8 %reduce-scatter.38.cloned.1.call-done = f32[120,640]{1,0:T(8,128)} async-done(((f32[960,640]{1,0:T(8,128)}), f32[120,640]{1,0:T(8,128)}) %reduce-scatter.38.cloned.1.call-update) | async-done | bytes 307216
  1501.5 66.6 %reduce-scatter.32.cloned.1.call-done = f32[120,240]{1,0:T(8,128)} async-done(((f32[960,240]{1,0:T(8,128)}), f32[120,240]{1,0:T(8,128)}) %reduce-scatter.32.cloned.1.call-update) | async-done | bytes 115216 | tf_op jit(solution)/shard_map/reduce_scatter | solution.py:320
  (431 shorter events, 483.0 us)
Async XLA Ops:
  8.0 74.8 %all-gather.11.cloned.1.call-start = ((), (), s32[]{:S(2)}) async-start(), calls=%async_computation.19 | async-start | bytes 4915200 | tf_op jit(solution)/shard_map/all_gather | solution.py:87
  47.3 366.6 %copy-start = (f32[512,960]{0,1:T(8,128)}, f32[512,960]{0,1:T(8,128)S(1)}, u32[]{:S(2)}) copy-start(f32[512,960]{0,1:T(8,128)S(1)} %copy.93) | copy-start | bytes 5898244
  88.4 25.2 %all-to-all-start.1 = ((bf16[4,512,400]{1,2,0:T(8,128)(2,1)}), bf16[4,512,400]{1,2,0:T(8,128)(2,1)}, u32[]{:S(2)}, u32[]{:S(2)}) async-start(bf16[4,512,400]{1,2,0:T(8,128)(2,1)} %bitcast.240), calls=%async_computation.1 | async-start | bytes 3276800 | tf_op jit(solution)/shard_map/all_to_all | solution.py:91
  92.8 40.0 %all-gather.13.cloned.1.call-start = ((), (), s32[]{:S(2)}) async-start(), calls=%async_computation.20 | async-start | bytes 1638400 | tf_op jit(solution)/shard_map/all_gather | solution.py:234
  116.4 36.8 %all-gather.15.cloned.1.call-start = ((), (), s32[]{:S(2)}) async-start(), calls=%async_computation.21 | async-start | bytes 1638400 | tf_op jit(solution)/shard_map/all_gather | solution.py:235
  157.0 149.7 %copy-start.24 = (bf16[120,240]{1,0:T(8,128)(2,1)S(1)}, bf16[120,240]{1,0:T(8,128)(2,1)}, u32[]{:S(2)}) copy-start(bf16[120,240]{1,0:T(8,128)(2,1)} %param.21) | copy-start | bytes 172804
  303.1 35.1 %all-to-all-start.2 = ((bf16[512,4,240]{0,2,1:T(8,128)(2,1)}), bf16[512,4,240]{0,2,1:T(8,128)(2,1)S(1)}, u32[]{:S(2)}, u32[]{:S(2)}) async-start(bf16[512,4,240]{0,2,1:T(8,128)(2,1)} %bitcast.20), calls=%async_computation.2 | async-start | bytes 1966080 | tf_op jit(solution)/shard_map/all_to_all | solution.py:95
  306.6 107.3 %reduce-scatter.20.cloned.1.call-start = ((), (), s32[]{:S(2)}) async-start(), calls=%async_computation.22 | async-start | bytes 9830400 | tf_op jit(solution)/shard_map/reduce_scatter | solution.py:102
  343.5 107.5 %all-gather.21.cloned.1.call-start = ((), (), s32[]{:S(2)}) async-start(), calls=%async_computation.25 | async-start | bytes 1382400 | tf_op jit(solution)/shard_map/all_gather | solution.py:207
  344.1 73.1 %copy-start.23 = (f32[960]{0:T(1024)S(1)}, f32[960]{0:T(1024)}, u32[]{:S(2)}) copy-start(f32[960]{0:T(1024)} %param.22) | copy-start | bytes 11524
  344.1 107.2 %all-gather.17.cloned.1.call-start = ((), (), s32[]{:S(2)}) async-start(), calls=%async_computation.23 | async-start | bytes 4915200 | tf_op jit(solution)/shard_map/all_gather | solution.py:87
  418.4 76.9 %all-gather.19.cloned.1.call-start = ((), (), s32[]{:S(2)}) async-start(), calls=%async_computation.24 | async-start | bytes 1382400 | tf_op jit(solution)/shard_map/all_gather | solution.py:206
  419.0 119.2 %all-gather.23.cloned.1.call-start = ((), (), s32[]{:S(2)}) async-start(), calls=%async_computation.26 | async-start | bytes 1382400 | tf_op jit(solution)/shard_map/all_gather | solution.py:208
  419.7 153.2 %all-gather.25.cloned.1.call-start = ((), (), s32[]{:S(2)}) async-start(), calls=%async_computation.28 | async-start | bytes 5242880 | tf_op jit(solution)/shard_map/all_gather | solution.py:87
  450.9 210.1 %reduce-scatter.24.cloned.1.call-start = ((), (), s32[]{:S(2)}) async-start(), calls=%async_computation.29 | async-start | bytes 9830400 | tf_op jit(solution)/shard_map/reduce_scatter | solution.py:102
  503.6 79.8 %copy-start.31 = (bf16[960,640]{1,0:T(8,128)(2,1)S(1)}, bf16[960,640]{1,0:T(8,128)(2,1)}, u32[]{:S(2)}) copy-start(bf16[960,640]{1,0:T(8,128)(2,1)} %all-gather.19.cloned.1.call-done) | copy-start | bytes 3686404
  592.1 69.0 %copy-start.3 = (f32[512,960]{0,1:T(8,128)S(1)}, f32[512,960]{0,1:T(8,128)}, u32[]{:S(2)}) copy-start(f32[512,960]{0,1:T(8,128)} %copy-done.2) | copy-start | bytes 5898244
  592.1 105.9 %all-gather.27.cloned.1.call-start = ((), (), s32[]{:S(2)}) async-start(), calls=%async_computation.30 | async-start | bytes 4915200 | tf_op jit(solution)/shard_map/all_gather | solution.py:87
  594.6 68.8 %copy-start.6 = (bf16[512,960]{0,1:T(8,128)(2,1)S(1)}, bf16[512,960]{0,1:T(8,128)(2,1)}, u32[]{:S(2)}) copy-start(bf16[512,960]{0,1:T(8,128)(2,1)} %copy.96) | copy-start | bytes 2949124
  702.4 17.2 %all-to-all-start.5 = ((bf16[4,512,240]{1,2,0:T(8,128)(2,1)}), bf16[4,512,240]{1,2,0:T(8,128)(2,1)S(1)}, u32[]{:S(2)}, u32[]{:S(2)}) async-start(bf16[4,512,240]{1,2,0:T(8,128)(2,1)} %bitcast.164), calls=%async_computation.8 | async-start | bytes 1966080 | tf_op jit(solution)/shard_map/all_to_all | solution.py:91
  705.9 283.0 %reduce-scatter.26.cloned.1.call-start = ((), (), s32[]{:S(2)}) async-start(), calls=%async_computation.31 | async-start | bytes 1638400 | tf_op jit(solution)/shard_map/reduce_scatter | solution.py:295
  962.3 56.0 %reduce-scatter.28.cloned.1.call-start = ((), (), s32[]{:S(2)}) async-start(), calls=%async_computation.32 | async-start | bytes 1638400 | tf_op jit(solution)/shard_map/reduce_scatter | solution.py:298
  963.7 153.6 %reduce-scatter.30.cloned.1.call-start = ((), (), s32[]{:S(2)}) async-start(), calls=%async_computation.33 | async-start | bytes 9830400 | tf_op jit(solution)/shard_map/reduce_scatter | solution.py:102
  1048.3 140.5 %reduce-scatter.22.cloned.1.call-start = ((), (), s32[]{:S(2)}) async-start(), calls=%async_computation.27 | async-start | bytes 9830400 | tf_op jit(solution)/shard_map/reduce_scatter | solution.py:102
  1057.5 222.8 %reduce-scatter.34.cloned.1.call-start = ((), (), s32[]{:S(2)}) async-start(), calls=%async_computation.35 | async-start | bytes 2211840
  1064.0 289.9 %reduce-scatter.40.cloned.1.call-start = ((), (), s32[]{:S(2)}) async-start(), calls=%async_computation.38 | async-start | bytes 2764800
  1072.2 355.4 %reduce-scatter.36.cloned.1.call-start = ((), (), s32[]{:S(2)}) async-start(), calls=%async_computation.36 | async-start | bytes 2764800
  1080.3 421.2 %reduce-scatter.38.cloned.1.call-start = ((), (), s32[]{:S(2)}) async-start(), calls=%async_computation.37 | async-start | bytes 2764800
  1087.1 101.6 %copy-start.7 = (bf16[512,960]{0,1:T(8,128)(2,1)S(1)}, bf16[512,960]{0,1:T(8,128)(2,1)}, u32[]{:S(2)}) copy-start(bf16[512,960]{0,1:T(8,128)(2,1)} %copy.96) | copy-start | bytes 2949124
  1195.8 44.9 %all-to-all-start.7 = ((bf16[8,64,960]{2,1,0:T(8,128)(2,1)}), bf16[8,64,960]{2,1,0:T(8,128)(2,1)S(1)}, u32[]{:S(2)}, u32[]{:S(2)}) async-start(bf16[8,64,960]{2,1,0:T(8,128)(2,1)} %bitcast.42), calls=%async_computation.13 | async-start | bytes 2097152 | tf_op jit(solution)/shard_map/all_to_all | solution.py:328
  1240.8 68.3 %all-to-all-start.3 = ((bf16[8,64,960]{2,1,0:T(8,128)(2,1)}), bf16[8,64,960]{2,1,0:T(8,128)(2,1)S(1)}, u32[]{:S(2)}, u32[]{:S(2)}) async-start(bf16[8,64,960]{2,1,0:T(8,128)(2,1)} %bitcast.22), calls=%async_computation.5 | async-start | bytes 2097152 | tf_op jit(solution)/shard_map/all_to_all | solution.py:327
  1244.3 323.8 %reduce-scatter.32.cloned.1.call-start = ((), (), s32[]{:S(2)}) async-start(), calls=%async_computation.34 | async-start | bytes 1105920 | tf_op jit(solution)/shard_map/reduce_scatter | solution.py:320
  (28 other events, 345.1 us)
Sparse Core Ops, SparseCore 0:
  48.8 32.0 all-gather.10
  116.5 16.2 all-gather.12
  134.9 18.1 all-gather.14
  343.6 70.1 reduce-scatter.19
  665.0 32.9 all-gather.26
  962.4 26.5 reduce-scatter.25
  991.7 26.5 reduce-scatter.27
Sparse Core Ops, SparseCore 1:
  346.1 42.9 all-gather.20
  418.5 32.8 all-gather.16
  453.6 41.7 all-gather.18
  497.8 40.4 all-gather.22
  539.9 33.0 all-gather.24
  592.2 68.8 reduce-scatter.23
  1048.3 68.9 reduce-scatter.29
  1119.8 68.8 reduce-scatter.21
  1192.1 88.1 reduce-scatter.33
  1284.9 69.0 reduce-scatter.39
  1358.5 69.2 reduce-scatter.35
  1432.3 69.1 reduce-scatter.37
  1505.6 62.4 reduce-scatter.31
